TPU v7x, 32 devices: a whole 2x2x4 slice. The times are simulated.
32 devices in a mesh: groups: 2 (over y), expert: 8 (over z, core), sub: 2 (over x).
Axes of the slice: x: 2, y: 2, z: 4, core: 2. Of those that a mesh axis runs over, the one named last changes fastest.
Arguments:
- latent: bfloat16 [4096, 1024], P(('groups', 'expert', 'sub')), parts along dimension 0, may hold values from -6 to 6
- routes: int32 [4096, 4], P(('groups', 'expert', 'sub')), parts along dimension 0, may hold values from 0 to 7, all different within a row; in each aligned block of 128 rows (0 to 127, 128 to 255, ...) at most 96 rows name the same one
- gates: float32 [4096, 4], P(('groups', 'expert', 'sub')), parts along dimension 0, may hold values from 0.1 to 1
- up_weight: bfloat16 [8, 1024, 2688], P('expert', None, 'sub'), may hold values from -0.1875 to 0.1875
- down_weight: bfloat16 [8, 1024, 2688], P('expert', None, 'sub'), may hold values from -0.125 to 0.125
Outputs:
- mixed: bfloat16 [4096, 1024], P(('groups', 'expert', 'sub')), parts along dimension 0
There are 2 independent parts, one for each index of `groups`. A program takes and returns all parts, laid end to end along the dimension named above; an argument that names none is the same for every part. Nothing has to cross between parts.
Inputs may be any that keep to these rules, and one draw needn't show every extreme that they name: `routes`: each token names 4 different experts; among the 128 tokens of one device no expert is named more than 96 times, a bound that some block reaches.
All inputs are finite; a program needn't handle non-finite values.
Results may differ from a plain program's by a relative error of at most 0.0058.
Values may be sent and summed in bfloat16 or wider, within the bound.
A program may use at most 128 MiB of HBM per device.

v0:
```python
import functools

import jax
import jax.numpy as jnp
from jax import lax
from jax.experimental import pallas as pl
from jax.experimental.pallas import tpu as pltpu
from jax.sharding import PartitionSpec as P

CORES = 2
PIECES = 2
VMEM_MOST = 60 * 1024 * 1024
F32, BF16 = jnp.float32, jnp.bfloat16


def expert_part(row_block, up_part, down_part):
    preact = jnp.dot(row_block, up_part, preferred_element_type=F32)
    active = jnp.square(jnp.maximum(preact, 0.0)).astype(BF16)
    return lax.dot_general(
        active, down_part, (((1,), (1,)), ((), ())), preferred_element_type=F32
    )


def routed(latent, routes, gates, up_weight, down_weight):
    tokens_here, row_width = latent.shape
    top_count = routes.shape[1]
    experts = lax.axis_size("expert")
    slot_most = min(tokens_here, 3 * tokens_here * top_count // (2 * experts))
    pair_count = tokens_here * top_count
    route_ids = routes.reshape(-1)
    one_hot = (route_ids[:, None] == jnp.arange(experts, dtype=jnp.int32)[None, :]).astype(
        jnp.int32
    )
    before = jnp.cumsum(one_hot, axis=0) - one_hot
    slot_rank = jnp.sum(before * one_hot, axis=1)
    slot_of = route_ids * slot_most + slot_rank
    source = (
        jnp.full((experts * slot_most,), pair_count, jnp.int32)
        .at[slot_of]
        .set(jnp.arange(pair_count, dtype=jnp.int32))
    )
    padded = jnp.concatenate([latent, jnp.zeros((1, row_width), latent.dtype)], axis=0)
    send_rows = padded[source // top_count].reshape(experts, slot_most, row_width)
    arrived = lax.all_to_all(send_rows, "expert", split_axis=0, concat_axis=0, tiled=True)
    flat_rows = arrived.reshape(-1, row_width)
    summed = expert_part(
        flat_rows,
        lax.all_gather(up_weight, "sub", axis=2, tiled=True)[0],
        lax.all_gather(down_weight, "sub", axis=2, tiled=True)[0],
    )
    expert_out = lax.all_to_all(
        summed.astype(BF16).reshape(arrived.shape),
        "expert",
        split_axis=0,
        concat_axis=0,
        tiled=True,
    )
    values = expert_out.reshape(experts * slot_most, row_width)[slot_of].astype(F32)
    mixed_out = jnp.sum(
        values.reshape(tokens_here, top_count, row_width) * gates[:, :, None], axis=1
    )
    return mixed_out.astype(BF16)


def team_kernel(
    lanes,
    latent_ref, share_ref, up_hbm, down_hbm, out_ref,
    rows, shares, up, down, kept, sib_out, sib_in, x_out, x_in, lane_out, lane_in,
    w_sem, lane_s, lane_r, x_s, x_r, sib_s, sib_r,
    rsib_s, rsib_r, rx_s, rx_r, rlane_s, rlane_r, next_s, mid_r, lane_mid, lane_sum,
):
    tokens = latent_ref.shape[0]
    me = lax.axis_index("expert")
    sub = lax.axis_index("sub")
    chip, core = me // CORES, me % CORES
    sibling = {"expert": chip * CORES + 1 - core}
    partner = {"sub": 1 - sub}
    bits = lanes.bit_length() - 1

    def lane_peer(step):
        place = 0
        for bit in range(bits):
            size = 1 << bit
            place = place + size * ((chip // size + step // size) % 2)
        return {"expert": place * CORES + core}

    def send(src, dst, s_sem, r_sem, device):
        return pltpu.make_async_remote_copy(
            src_ref=src, dst_ref=dst, send_sem=s_sem, recv_sem=r_sem,
            device_id=device, device_id_type=pl.DeviceIdType.MESH,
        )

    own = (latent_ref, share_ref)
    boxes = (rows, shares)

    def to_lane(kind, step, hops=None, src=None, slot=None):
        hops = step if hops is None else hops
        src = own[kind] if src is None else boxes[kind].at[0, src, 0]
        slot = step if slot is None else slot
        return send(src, boxes[kind].at[0, step, 0], lane_s.at[kind, slot],
                    lane_r.at[kind, step], lane_peer(hops))

    relay = lanes == 4
    inner = ((chip + 1) // 2) % 2 == 1

    def relayed(kind, what):
        if what == 0:
            return to_lane(kind, 2, 3, 1, 2)
        if what == 1:
            return to_lane(kind, 2, 1, 3, 4)
        return to_lane(kind, 3, 1, 2, 5)

    def to_sub(kind, step, src=None):
        src = boxes[kind].at[0, step, 0] if src is None else src
        return send(src, boxes[kind].at[1, step, 0], x_s.at[kind, step],
                    x_r.at[kind, step], partner)

    around = 2 * jnp.where(inner, 1, 0)

    def crossing(step):
        return jnp.where(inner & (step == 1), 3, step)

    def to_next(kind):
        return send(boxes[kind].at[1, around, 0], boxes[kind].at[1, around + 1, 0],
                    next_s.at[kind], x_r.at[kind, around + 1], lane_peer(1))

    def to_sibling(kind, other, step, src=None):
        src = boxes[kind].at[other, step, 0] if src is None else src
        return send(src, boxes[kind].at[other, step, 1], sib_s.at[kind, other, step],
                    sib_r.at[kind, other, step], sibling)

    def back_sibling(other, step):
        return send(sib_out.at[other, step], sib_in.at[other, step], rsib_s.at[other, step],
                    rsib_r.at[other, step], sibling)

    def back_sub(step, piece):
        return send(x_out.at[step, piece], x_in.at[step, piece], rx_s.at[step, piece],
                    rx_r.at[step, piece], partner)

    def back_lane(step, piece, src=None):
        src = lane_out if src is None else src
        return send(src.at[step, piece], lane_in.at[step, piece],
                    rlane_s.at[step, piece], rlane_r.at[step, piece], lane_peer(step))

    def to_inner(step, piece):
        return send(lane_out.at[step, piece], lane_mid.at[5 - step, piece],
                    rlane_s.at[step, piece], mid_r.at[5 - step, piece], lane_peer(1))

    def span(piece):
        return pl.ds(piece * (tokens // PIECES), tokens // PIECES)

    up_copy = pltpu.make_async_copy(up_hbm.at[0], up, w_sem.at[0])
    down_copy = pltpu.make_async_copy(down_hbm.at[0], down, w_sem.at[1])
    up_copy.start()
    down_copy.start()

    barrier = pltpu.get_barrier_semaphore()
    greeted = [sibling, partner] + [lane_peer(step) for step in range(1, lanes)]
    for device in greeted:
        pl.semaphore_signal(barrier, inc=1, device_id=device,
                            device_id_type=pl.DeviceIdType.MESH)
    pl.semaphore_wait(barrier, len(greeted))

    for kind in (1, 0):
        to_sub(kind, 0, own[kind]).start()
        to_sibling(kind, 0, 0, own[kind]).start()
        if relay:
            to_lane(kind, 1).start()

            @pl.when(inner)
            def _():
                to_lane(kind, 3).start()
        else:
            for step in range(1, lanes):
                to_lane(kind, step).start()
    rows[0, 0, 0] = latent_ref[...]
    shares[0, 0, 0] = share_ref[...]
    up_copy.wait()
    down_copy.wait()

    def finish_sub(step):
        back_sibling(1, step).wait_recv()
        for piece in range(PIECES):
            total = kept[1, step, span(piece)] + sib_in[1, step, span(piece)].astype(F32)
            x_out[step, piece] = total.astype(BF16)
            back_sub(step, piece).start()

    def gate_column(other, step, side):
        line = shares[other, step, side, me]
        spot = lax.broadcasted_iota(jnp.int32, (tokens, tokens), 0) == lax.broadcasted_iota(
            jnp.int32, (tokens, tokens), 1
        )
        return jnp.sum(jnp.where(spot, line, 0.0), axis=1, keepdims=True)

    def one(index, carry):
        step, other = index // 2, index % 2

        @pl.when((other == 1) & (step + 1 < lanes))
        def _():
            if relay:
                @pl.when(jnp.logical_not(inner & (step == 2)))
                def _():
                    for kind in (0, 1):
                        to_lane(kind, step + 1).wait_recv()

                @pl.when(inner & (step == 0))
                def _():
                    for kind in (0, 1):
                        relayed(kind, 0).start()
                    for kind in (0, 1):
                        to_lane(kind, 3).wait_recv()
                        relayed(kind, 1).start()

                @pl.when(inner & (step == 1))
                def _():
                    for kind in (0, 1):
                        relayed(kind, 2).start()
            else:
                for kind in (0, 1):
                    to_lane(kind, step + 1).wait_recv()
            for kind in (0, 1):
                if relay:
                    @pl.when(step < 2)
                    def _():
                        to_sub(kind, crossing(step + 1)).start()
                else:
                    to_sub(kind, step + 1).start()
                to_sibling(kind, 0, step + 1).start()

        @pl.when(other == 1)
        def _():
            for kind in (0, 1):
                to_sub(kind, step).wait_recv()
                if relay:
                    @pl.when(step == around)
                    def _():
                        to_next(kind).start()
                to_sibling(kind, 1, step).start()

        for kind in (0, 1):
            to_sibling(kind, other, step).wait_recv()
        block = rows[other, step].reshape(2 * tokens, rows.shape[-1])
        preact = lax.dot_general(
            block, up[...], (((1,), (1,)), ((), ())), preferred_element_type=F32
        )
        active = jnp.square(jnp.maximum(preact, 0.0)).astype(BF16)
        part = jnp.dot(active, down[...], preferred_element_type=F32)
        kept[other, step] = part[:tokens] * gate_column(other, step, 0)
        sib_out[other, step] = (part[tokens:] * gate_column(other, step, 1)).astype(BF16)
        back_sibling(other, step).start()

        @pl.when((other == 0) & (step >= 3))
        def _():
            finish_sub(step - 1)

        return carry

    lax.fori_loop(0, 2 * lanes, one, 0)

    for step in (*range(min(lanes, 3) - 1, 0, -1), 0) if lanes < 4 else (lanes - 1, 1, 0):
        finish_sub(step)

    def column_total(step, piece):
        back_sub(step, piece).wait_recv()
        total = kept[0, step, span(piece)] + sib_in[0, step, span(piece)].astype(F32)
        return total + x_in[step, piece].astype(F32)

    for step in range(lanes):
        back_sibling(0, step).wait_recv()
    def returned(step, piece):
        if not relay or step == 1:
            back_lane(step, piece).start()
            return

        @pl.when(inner)
        def _():
            to_inner(5 - step, piece).wait_recv()
            total = lane_out[step, piece].astype(F32) + lane_mid[step, piece].astype(F32)
            lane_sum[step, piece] = total.astype(BF16)
            back_lane(step, piece, lane_sum).start()

        @pl.when(jnp.logical_not(inner))
        def _():
            to_inner(step, piece).start()

    for step in (*range(2, lanes), 1) if lanes > 1 else ():
        for piece in range(PIECES):
            lane_out[step, piece] = column_total(step, piece).astype(BF16)
            returned(step, piece)
    near = 2 + jnp.where(inner, 1, 0)
    for piece in range(PIECES):
        total = column_total(0, piece)
        for step in (1, near) if relay else range(1, lanes):
            back_lane(step, piece).wait_recv()
            total = total + lane_in[step, piece].astype(F32)
        out_ref[span(piece), :] = total.astype(BF16)

    for step in range(lanes):
        for kind in (0, 1):
            if not relay:
                to_sub(kind, step).wait_send()
            elif step < 3:
                to_sub(kind, crossing(step)).wait_send()
            else:
                to_next(kind).wait_send()
            for other in (0, 1):
                to_sibling(kind, other, step).wait_send()
            if step == 1 or (step and not relay):
                to_lane(kind, step).wait_send()
        for other in (0, 1):
            back_sibling(other, step).wait_send()
        for piece in range(PIECES):
            back_sub(step, piece).wait_send()
            if step:
                back_lane(step, piece).wait_send()
    if relay:
        @pl.when(inner)
        def _():
            for kind in (0, 1):
                to_lane(kind, 3).wait_send()
                for what in range(3):
                    relayed(kind, what).wait_send()


def team(latent, routes, gates, up_weight, down_weight):
    tokens, width = latent.shape
    hidden = up_weight.shape[2]
    experts = lax.axis_size("expert")
    lanes = experts // CORES
    chosen = routes[None, :, :] == jnp.arange(experts, dtype=jnp.int32)[:, None, None]
    share = jnp.sum(jnp.where(chosen, gates[None, :, :], 0.0), axis=2).reshape(experts, 1, tokens)
    vmem = pl.BlockSpec(memory_space=pltpu.VMEM)
    hbm = pl.BlockSpec(memory_space=pl.ANY)
    dma = pltpu.SemaphoreType.DMA
    return pl.pallas_call(
        functools.partial(team_kernel, lanes),
        out_shape=jax.ShapeDtypeStruct((tokens, width), BF16),
        in_specs=[vmem, vmem, hbm, hbm],
        out_specs=vmem,
        scratch_shapes=[
            pltpu.VMEM((2, lanes, 2, tokens, width), BF16),
            pltpu.VMEM((2, lanes, 2, experts, 1, tokens), F32),
            pltpu.VMEM((hidden, width), BF16),
            pltpu.VMEM((hidden, width), BF16),
            pltpu.VMEM((2, lanes, tokens, width), F32),
            pltpu.VMEM((2, lanes, tokens, width), BF16),
            pltpu.VMEM((2, lanes, tokens, width), BF16),
            pltpu.VMEM((lanes, PIECES, tokens // PIECES, width), BF16),
            pltpu.VMEM((lanes, PIECES, tokens // PIECES, width), BF16),
            pltpu.VMEM((lanes, PIECES, tokens // PIECES, width), BF16),
            pltpu.VMEM((lanes, PIECES, tokens // PIECES, width), BF16),
            dma((2,)),
            dma((2, lanes + 2)), dma((2, lanes)), dma((2, lanes)), dma((2, lanes)),
            dma((2, 2, lanes)), dma((2, 2, lanes)),
            dma((2, lanes)), dma((2, lanes)),
            dma((lanes, PIECES)), dma((lanes, PIECES)), dma((lanes, PIECES)), dma((lanes, PIECES)),
            dma((2,)),
            dma((lanes, PIECES)),
            pltpu.VMEM((lanes, PIECES, tokens // PIECES, width), BF16),
            pltpu.VMEM((lanes, PIECES, tokens // PIECES, width), BF16),
        ],
        compiler_params=pltpu.CompilerParams(
            collective_id=0, has_side_effects=True, vmem_limit_bytes=VMEM_MOST
        ),
    )(latent, share, jnp.swapaxes(up_weight, 1, 2), jnp.swapaxes(down_weight, 1, 2))


def local(latent, routes, gates, up_weight, down_weight):
    tokens, width = latent.shape
    experts, subs = lax.axis_size("expert"), lax.axis_size("sub")
    lanes = experts // CORES
    block = tokens * width * 2
    need = block * lanes * (4 + 4 + 2 + 2 + 4) + 4 * up_weight.size + 16 * block
    fits = subs == 2 and lanes & (lanes - 1) == 0 and need < VMEM_MOST
    plan = team if fits and experts % CORES == 0 and tokens % 128 == 0 else routed
    return plan(latent, routes, gates, up_weight, down_weight)


def solution(mesh):
    placed = (
        P(("groups", "expert", "sub"), None),
        P(("groups", "expert", "sub"), None),
        P(("groups", "expert", "sub"), None),
        P("expert", None, "sub"),
        P("expert", None, "sub"),
    )
    return jax.shard_map(
        local,
        mesh=mesh,
        in_specs=placed,
        out_specs=P(("groups", "expert", "sub"), None),
        check_vma=False,
    )
```

profile of v0, /device:TPU:0, one launch (start us, length us, event | category | flops | bytes accessed | tf_op | source)
XLA Modules:
  0.0 65.8 jit_solution(9391852750029788177)
XLA Ops:
  0.0 1.3 %select_reduce_fusion = f32[8,128]{1,0:T(8,128)} fusion(f32[128,4]{0,1:T(4,128)} %param.7, s32[128,4]{0,1:T(4,128)} %param.6), kind=kLoop, calls=%fused_computation | loop fusion | flops 11264 | bytes 8192 | tf_op jit(solution)/shard_map/reduce_sum | solution.py:331
  1.3 62.9 %shard_map.55 = bf16[128,1024]{1,0:T(8,128)(2,1)} custom-call(bf16[128,1024]{1,0:T(8,128)(2,1)} %latent_ref.1, f32[8,1,128]{2,1,0:T(1,128)} %bitcast.5, bf16[1,1344,1024]{2,1,0:T(8,128)(2,1)} %bitcast.3, bf16[1,1344,1024]{2,1,0:T(8,128)(2,1)} %bitcast.4), custom_call_target="tpu_custom_call" | custom-call | tf_op jit(solution)/shard_map/pallas_call | solution.py:335
  64.2 1.7 %copy.9 = bf16[128,1024]{1,0:T(8,128)(2,1)} copy(bf16[128,1024]{1,0:T(8,128)(2,1)} %shard_map.55) | data formatting | bytes 524288
where the time goes:
time: 66 us; the launch traced here: 65.8 us
  Pallas kernels  62.9 us (95%)
  local copies, waits for them, and re-layouts  1.67 us (3%)
  other arithmetic  1.3 us (2%)
    pallas_call x1, Pallas kernels, team(): pl.pallas_call(functools.partial(team_kernel, lanes), out_shape=jax.Shape...  62.9 us
    unnamed x1, local copies, waits for them, and re-layouts  1.67 us

commit v1 on v0

v1 whole, which is shorter than its diff:
```python
import jax
import jax.numpy as jnp
from jax import lax
from jax.experimental import pallas as pl
from jax.experimental.pallas import tpu as pltpu
from jax.sharding import PartitionSpec as P

CORES = 2
PIECES = 4
VMEM_MOST = 60 * 1024 * 1024
F32, BF16 = jnp.float32, jnp.bfloat16


END_UNITS = (
    (0, 1, 2, 3),
    (4, 5, 17, 18),
    (21, 8, 6, 16),
    (20, 24, 12, 10),
    (25, 28, 14, 19),
    (26, 29, 30, 31),
    (22, 27, 13, 15),
    (23, 9, 11, 7),
)
END_MOVES = (
    (
        (0, 0), (0, 1), (0, 2), (0, 3), (1, 0, 1, 1), (1, 2, 1, 1), (1, 1, 0, 4), (1, 2, 0, 4), (1, 3, 1, 1),
        (1, 0, 0, 4), (1, 1, 1, 1),
    ),
    (
        (0, 5), (0, 17), (0, 4), (0, 18), (1, 17, 1, 5), (1, 5, 0, 5), (1, 3, 0, 4), (1, 18, 1, 5), (0, 6),
        (0, 16),
    ),
    (
        (0, 21), (0, 8), (1, 8, 0, 6), (0, 19), (0, 20), (2, 17, 0, 0, 0), (2, 4, 1, 0, 0), (2, 5, 1, 0, 0),
    ),
    (
        (0, 10), (0, 24), (0, 12), (1, 12, 0, 7), (1, 10, 0, 6), (0, 25), (2, 16, 0, 0, 0), (2, 8, 1, 3, 0),
        (2, 21, 1, 4, 0),
    ),
    (
        (0, 14), (0, 28), (1, 14, 0, 7), (0, 15), (0, 26), (2, 24, 1, 7, 0), (2, 20, 1, 4, 0), (0, 29),
    ),
    (
        (0, 31), (0, 30), (0, 11), (1, 11, 0, 6), (2, 28, 0, 3, 0), (2, 14, 1, 2, 0), (2, 25, 1, 7, 0),
    ),
    (
        (0, 13), (0, 27), (0, 22), (2, 12, 1, 2, 1), (0, 23), (2, 29, 0, 3, 0), (2, 30, 1, 6, 0),
        (2, 26, 0, 2, 0),
    ),
    (
        (0, 7), (0, 9), (2, 31, 1, 6, 0), (2, 13, 1, 2, 1), (2, 15, 1, 2, 0), (2, 27, 0, 2, 0),
        (2, 22, 0, 1, 0),
    ),
    (
        (2, 10, 1, 3, 1), (2, 9, 1, 3, 0), (2, 11, 1, 3, 1), (2, 23, 0, 1, 0), (2, 0, 3, 0, 3),
        (2, 6, 1, 0, 1), (2, 18, 0, 0, 2), (2, 7, 1, 0, 1), (2, 19, 0, 0, 2), (2, 1, 3, 0, 3),
        (2, 2, 3, 0, 3), (2, 3, 3, 0, 3),
    ),
)
INNER_UNITS = (
    (0, 1, 2, 3),
    (12, 13, 4, 6),
    (14, 16, 18, 19),
    (8, 15, 5, 7),
    (10, 21, 22, 23),
    (11, 24, 25, 20),
    (26, 27, 17, 28),
    (9, 29, 30, 31),
)
INNER_MOVES = (
    (
        (0, 0), (0, 1), (0, 2), (0, 3), (1, 0, 2, 3), (1, 1, 2, 3), (1, 1, 1, 1), (1, 0, 1, 1), (1, 0, 0, 4),
        (1, 2, 0, 4), (1, 2, 2, 3), (1, 2, 1, 1), (1, 3, 0, 4), (1, 3, 2, 3),
    ),
    (
        (0, 4), (0, 12), (0, 6), (0, 13), (0, 16), (0, 18), (1, 13, 0, 7), (1, 12, 0, 7), (1, 4, 2, 2),
        (1, 12, 1, 2), (1, 16, 1, 5), (1, 6, 2, 2), (0, 7), (0, 14), (0, 19), (1, 7, 0, 5), (1, 14, 1, 2),
    ),
    (
        (0, 15), (0, 5), (0, 21), (0, 29), (0, 8), (1, 8, 1, 3), (1, 21, 2, 6), (1, 8, 0, 6), (1, 7, 2, 2),
        (1, 29, 1, 6), (1, 4, 0, 5),
    ),
    (
        (0, 28), (0, 10), (0, 22), (0, 23), (1, 10, 1, 3), (1, 23, 2, 6), (1, 22, 2, 6), (1, 1, 0, 4),
    ),
    (
        (0, 25), (0, 24), (0, 11), (0, 20), (1, 11, 1, 3), (1, 5, 2, 2), (1, 25, 1, 7), (2, 18, 0, 0, 0),
    ),
    (
        (0, 27), (0, 26), (0, 17), (1, 27, 1, 7), (1, 15, 1, 2), (1, 18, 2, 7), (1, 19, 2, 7),
    ),
    (
        (0, 9), (1, 9, 1, 3), (2, 12, 2, 0, 2), (2, 21, 0, 1, 0),
    ),
    (
        (0, 30), (0, 31), (1, 18, 1, 5), (1, 19, 1, 5), (2, 24, 2, 5, 0), (2, 25, 0, 2, 0), (1, 3, 1, 1),
        (2, 28, 2, 4, 2), (2, 17, 0, 0, 2),
    ),
    (
        (2, 20, 0, 1, 4), (2, 10, 2, 1, 2), (1, 13, 1, 2), (2, 16, 0, 0, 6), (2, 30, 0, 3, 0),
        (2, 31, 2, 4, 0), (2, 29, 0, 3, 2), (2, 6, 1, 0, 4), (2, 8, 2, 1, 2), (2, 0, 3, 0, 7),
        (2, 19, 0, 0, 4), (2, 26, 2, 5, 2), (2, 27, 2, 5, 2), (2, 4, 1, 0, 5), (2, 9, 2, 1, 3),
        (2, 22, 1, 4, 4), (2, 11, 2, 1, 2), (2, 23, 1, 4, 4), (2, 14, 2, 0, 3), (2, 5, 1, 0, 5),
        (2, 13, 2, 0, 3), (2, 7, 1, 0, 4), (2, 15, 2, 0, 2), (2, 2, 3, 0, 7), (2, 1, 3, 0, 7),
        (2, 3, 3, 0, 7),
    ),
)


def expert_part(row_block, up_part, down_part):
    preact = jnp.dot(row_block, up_part, preferred_element_type=F32)
    active = jnp.square(jnp.maximum(preact, 0.0)).astype(BF16)
    return lax.dot_general(
        active, down_part, (((1,), (1,)), ((), ())), preferred_element_type=F32
    )


def routed(latent, routes, gates, up_weight, down_weight):
    tokens_here, row_width = latent.shape
    top_count = routes.shape[1]
    experts = lax.axis_size("expert")
    slot_most = min(tokens_here, 3 * tokens_here * top_count // (2 * experts))
    pair_count = tokens_here * top_count
    route_ids = routes.reshape(-1)
    one_hot = (route_ids[:, None] == jnp.arange(experts, dtype=jnp.int32)[None, :]).astype(
        jnp.int32
    )
    before = jnp.cumsum(one_hot, axis=0) - one_hot
    slot_rank = jnp.sum(before * one_hot, axis=1)
    slot_of = route_ids * slot_most + slot_rank
    source = (
        jnp.full((experts * slot_most,), pair_count, jnp.int32)
        .at[slot_of]
        .set(jnp.arange(pair_count, dtype=jnp.int32))
    )
    padded = jnp.concatenate([latent, jnp.zeros((1, row_width), latent.dtype)], axis=0)
    send_rows = padded[source // top_count].reshape(experts, slot_most, row_width)
    arrived = lax.all_to_all(send_rows, "expert", split_axis=0, concat_axis=0, tiled=True)
    flat_rows = arrived.reshape(-1, row_width)
    summed = expert_part(
        flat_rows,
        lax.all_gather(up_weight, "sub", axis=2, tiled=True)[0],
        lax.all_gather(down_weight, "sub", axis=2, tiled=True)[0],
    )
    expert_out = lax.all_to_all(
        summed.astype(BF16).reshape(arrived.shape),
        "expert",
        split_axis=0,
        concat_axis=0,
        tiled=True,
    )
    values = expert_out.reshape(experts * slot_most, row_width)[slot_of].astype(F32)
    mixed_out = jnp.sum(
        values.reshape(tokens_here, top_count, row_width) * gates[:, :, None], axis=1
    )
    return mixed_out.astype(BF16)


def grid_kernel(
    routes_hbm, gates_hbm, latent_hbm, up_hbm, down_hbm, out_ref,
    routes, gates, mine, tables, rows, up, down, kept, mate_out, mate_in, sums_out, sums_in,
    small_sem, own_sem, w_sem, table_s, table_r, cross_s, cross_r,
    near_s, near_r, far_s, far_r, mate_s, mate_r, sum_s, sum_r,
):
    me = lax.axis_index("expert")
    sub = lax.axis_index("sub")
    chip, core = me // CORES, me % CORES
    lanes = tables.shape[1]
    experts = mine.shape[0]
    part = rows.shape[2]
    inner = ((chip + 1) // 2) % 2 == 1

    def place(step):
        first = (chip + step) % 2
        second = (chip // 2 + step // 2) % 2
        return first + 2 * second

    sibling = {"expert": chip * CORES + 1 - core}
    roads = ({"sub": 1 - sub}, {"expert": place(1) * CORES + core}, {"expert": place(3) * CORES + core})

    def send(src, dst, s_sem, r_sem, device):
        return pltpu.make_async_remote_copy(
            src_ref=src, dst_ref=dst, send_sem=s_sem, recv_sem=r_sem,
            device_id=device, device_id_type=pl.DeviceIdType.MESH,
        )

    small = [
        pltpu.make_async_copy(routes_hbm, routes, small_sem.at[0]),
        pltpu.make_async_copy(gates_hbm, gates, small_sem.at[1]),
    ]
    own = [
        pltpu.make_async_copy(latent_hbm.at[pl.ds(piece * part, part)], rows.at[piece, 0], own_sem.at[piece])
        for piece in range(PIECES)
    ]
    weights = [
        pltpu.make_async_copy(up_hbm.at[0], up, w_sem.at[0]),
        pltpu.make_async_copy(down_hbm.at[0], down, w_sem.at[1]),
    ]
    for copy in (*own, *small, *weights):
        copy.start()

    column = [
        (step, side) for step in range(lanes) for side in range(CORES) if step or side
    ]

    def table_peer(step, side):
        return place(step) * CORES + (core + side) % CORES

    barrier = pltpu.get_barrier_semaphore()
    greeted = [roads[0]] + [{"expert": table_peer(*who)} for who in column]
    for device in greeted:
        pl.semaphore_signal(barrier, inc=1, device_id=device, device_id_type=pl.DeviceIdType.MESH)
    for copy in (*small, *own):
        copy.wait()
    for expert in range(experts):
        mine[expert] = jnp.sum(
            jnp.where(routes[...] == expert, gates[...], 0.0), axis=0, keepdims=True
        )
    tables[0, 0, 0] = mine[me]
    pl.semaphore_wait(barrier, len(greeted))

    def to_column(step, side):
        return send(mine.at[table_peer(step, side)], tables.at[0, step, side], table_s,
                    table_r.at[step * CORES + side], {"expert": table_peer(step, side)})

    across = send(tables.at[0], tables.at[1], cross_s, cross_r, roads[0])

    def to_mate(code):
        return send(rows.at[code, 0], rows.at[code, 1], near_s, near_r.at[code], sibling)

    def onward(code, road, block):
        spot = block * PIECES + code % PIECES
        return send(rows.at[code, 0], rows.at[spot, 0], far_s, far_r.at[spot], roads[road])

    def part_to_mate(unit):
        return send(mate_out.at[unit], mate_in.at[unit], mate_s, mate_r.at[unit], sibling)

    def sum_onward(code, road, block):
        spot = block * PIECES + code % PIECES
        return send(sums_out.at[code], sums_in.at[3 * spot + road], sum_s, sum_r.at[spot, road], roads[road])

    def landed(code):
        onward(code, 0, code // PIECES).wait_recv()

    def run(units, phase, seen, joined):
        for move in phase:
            code = move[1]
            if move[0] < 2:
                if code >= PIECES and code not in seen:
                    landed(code)
                    seen.add(code)
                if move[0] == 0:
                    to_mate(code).start()
                else:
                    onward(code, move[2], move[3]).start()
                continue
            unit = [code in group for group in units].index(True)
            spot = units[unit].index(code)
            if unit not in joined:
                part_to_mate(unit).wait_recv()
                joined.add(unit)
            total = kept[unit, spot] + mate_in[unit, spot].astype(F32)
            for road in range(len(roads)):
                if move[4] >> road & 1:
                    sum_r_of = send(sums_out.at[code], sums_in.at[3 * code + road], sum_s,
                                    sum_r.at[code, road], roads[road])
                    sum_r_of.wait_recv()
                    total = total + sums_in[3 * code + road].astype(F32)
            if move[2] < len(roads):
                sums_out[code] = total.astype(BF16)
                sum_onward(code, *move[2:4]).start()
            else:
                out_ref[pl.ds(code * part, part)] = total.astype(BF16)

    plans = ((END_UNITS, END_MOVES), (INNER_UNITS, INNER_MOVES))
    known = ((set(), set()), (set(), set()))

    def both(phase, index):
        for role in (0, 1):
            @pl.when(inner == (role == 1))
            def _():
                units, moves = plans[role]
                run(units, moves[phase], *known[role])
                if phase < len(units):
                    for code in units[phase]:
                        to_mate(code).wait_recv()

    count = len(END_UNITS)
    width = len(END_UNITS[0])

    def lookup(index, spot):
        code = 0
        for unit in range(count):
            here = jnp.where(inner, INNER_UNITS[unit][spot], END_UNITS[unit][spot])
            code = jnp.where(index == unit, here, code)
        return code

    def gate_column(code, side):
        block, piece = code // PIECES, code % PIECES
        line = tables[block // lanes, block % lanes, side]
        row = lax.broadcasted_iota(jnp.int32, (part, line.shape[1]), 0) + piece * part
        lane = lax.broadcasted_iota(jnp.int32, (part, line.shape[1]), 1)
        return jnp.sum(jnp.where(row == lane, line, 0.0), axis=1, keepdims=True)

    def one(index, carry):
        for phase in range(count):
            @pl.when(index == phase)
            def _():
                if phase == 0:
                    for who in column:
                        to_column(*who).start()
                both(phase, index)
                if phase == 0:
                    for who in column:
                        to_column(*who).wait_recv()
                    across.start()
                    for copy in weights:
                        copy.wait()
                    across.wait_recv()

        codes = [lookup(index, spot) for spot in range(width)]
        block = jnp.concatenate([rows[code, side] for side in (0, 1) for code in codes], axis=0)
        preact = lax.dot_general(
            block, up[...], (((1,), (1,)), ((), ())), preferred_element_type=F32
        )
        active = jnp.square(jnp.maximum(preact, 0.0)).astype(BF16)
        result = jnp.dot(active, down[...], preferred_element_type=F32)
        for spot, code in enumerate(codes):
            near = result[spot * part:(spot + 1) * part]
            away = result[(width + spot) * part:(width + spot + 1) * part]
            kept[index, spot] = near * gate_column(code, 0)
            mate_out[index, spot] = (away * gate_column(code, 1)).astype(BF16)
        part_to_mate(index).start()
        return carry

    lax.fori_loop(0, count, one, 0)
    both(count, count)

    for who in column:
        to_column(*who).wait_send()
    across.wait_send()
    send(mate_out, mate_in, near_s, near_s, sibling).wait_send()
    send(mate_out, mate_in, mate_s, mate_s, sibling).wait_send()
    for role in (0, 1):
        @pl.when(inner == (role == 1))
        def _():
            moves = [move for phase in plans[role][1] for move in phase]
            for kind, sem in ((1, far_s), (2, sum_s)):
                sent = sum(move[0] == kind and move[2] < len(roads) for move in moves)
                whole = sums_in.at[pl.ds(0, sent)]
                send(whole, whole, sem, sem, roads[0]).wait_send()


def grid(latent, routes, gates, up_weight, down_weight):
    tokens, width = latent.shape
    top_count = routes.shape[1]
    hidden = up_weight.shape[2]
    experts = lax.axis_size("expert")
    lanes = experts // CORES
    blocks, part = 2 * lanes, tokens // PIECES
    units, spots = len(END_UNITS), len(END_UNITS[0])
    vmem = pl.BlockSpec(memory_space=pltpu.VMEM)
    hbm = pl.BlockSpec(memory_space=pl.ANY)
    dma = pltpu.SemaphoreType.DMA
    return pl.pallas_call(
        grid_kernel,
        out_shape=jax.ShapeDtypeStruct((tokens, width), BF16),
        in_specs=[hbm] * 5,
        out_specs=vmem,
        scratch_shapes=[
            pltpu.VMEM((top_count, tokens), jnp.int32),
            pltpu.VMEM((top_count, tokens), F32),
            pltpu.VMEM((experts, 1, tokens), F32),
            pltpu.VMEM((2, lanes, CORES, 1, tokens), F32),
            pltpu.VMEM((blocks * PIECES, 2, part, width), BF16),
            pltpu.VMEM((hidden, width), BF16),
            pltpu.VMEM((hidden, width), BF16),
            pltpu.VMEM((units, spots, part, width), F32),
            pltpu.VMEM((units, spots, part, width), BF16),
            pltpu.VMEM((units, spots, part, width), BF16),
            pltpu.VMEM((blocks * PIECES, part, width), BF16),
            pltpu.VMEM((blocks * PIECES * 3, part, width), BF16),
            dma((2,)), dma((PIECES,)), dma((2,)),
            dma, dma((lanes * CORES,)), dma, dma,
            dma, dma((blocks * PIECES,)), dma, dma((blocks * PIECES,)),
            dma, dma((units,)), dma, dma((blocks * PIECES, 3)),
        ],
        compiler_params=pltpu.CompilerParams(
            collective_id=0, has_side_effects=True, vmem_limit_bytes=VMEM_MOST
        ),
    )(routes.T, gates.T, latent, jnp.swapaxes(up_weight, 1, 2), jnp.swapaxes(down_weight, 1, 2))


def local(latent, routes, gates, up_weight, down_weight):
    tokens, width = latent.shape
    experts, subs = lax.axis_size("expert"), lax.axis_size("sub")
    block = tokens * width * 2
    need = 8 * block * (2 + 2 + 1 + 1 + 1 + 3) + 4 * up_weight.size + 4 * block
    fits = subs == 2 and experts == 4 * CORES and need < VMEM_MOST
    plan = grid if fits and tokens % (16 * PIECES) == 0 and tokens % 128 == 0 else routed
    return plan(latent, routes, gates, up_weight, down_weight)


def solution(mesh):
    placed = (
        P(("groups", "expert", "sub"), None),
        P(("groups", "expert", "sub"), None),
        P(("groups", "expert", "sub"), None),
        P("expert", None, "sub"),
        P("expert", None, "sub"),
    )
    return jax.shard_map(
        local,
        mesh=mesh,
        in_specs=placed,
        out_specs=P(("groups", "expert", "sub"), None),
        check_vma=False,
    )
```

time: 66 us -> 56.1 us (0.85)
  Pallas kernels: 62.9 us -> 54.2 us
  other arithmetic: 1.3 us -> 0 us
    pallas_call x1, Pallas kernels: 62.9 us -> 54.2 us  [grid(): pl.pallas_call(grid_kernel, out_shape=jax.ShapeDtypeStruct((tokens, width...]
    reduce_sum x1 -> x0, other arithmetic: 1.3 us -> none  [team(): jnp.sum(jnp.where(chosen, gates[None, :, :], 0.0), axis=2)]
where the time goes in v1:
time: 56.1 us; the launch traced here: 55.9 us
  Pallas kernels  54.2 us (97%)
  local copies, waits for them, and re-layouts  1.67 us (3%)
    pallas_call x1, Pallas kernels, grid(): pl.pallas_call(grid_kernel, out_shape=jax.ShapeDtypeStruct((tokens, width...  54.2 us
    unnamed x1, local copies, waits for them, and re-layouts  1.67 us

profile of v1, /device:TPU:0, one launch (start us, length us, event | category | flops | bytes accessed | tf_op | source)
XLA Modules:
  0.0 55.9 jit_solution(4210909333791736651)
XLA Ops:
  0.0 54.2 %shard_map.55 = bf16[128,1024]{1,0:T(8,128)(2,1)} custom-call(s32[4,128]{1,0:T(4,128)} %bitcast.6, f32[4,128]{1,0:T(4,128)} %bitcast.7, bf16[128,1024]{1,0:T(8,128)(2,1)} %latent_hbm.1, bf16[1,1344,1024]{2,1,0:T(8,128)(2,1)} %bitcast.4, bf16[1,1344,1024]{2,1,0:T(8,128)(2,1)} %bitcast.5), custom_call_target="tpu_custom_call" | custom-call | tf_op jit(solution)/shard_map/pallas_call | solution.py:365
  54.2 1.7 %copy.7 = bf16[128,1024]{1,0:T(8,128)(2,1)} copy(bf16[128,1024]{1,0:T(8,128)(2,1)} %shard_map.55) | data formatting | bytes 524288

commit v2 on v1

--- a/solution.py
+++ b/solution.py
@@ -7,102 +7,105 @@
 
 CORES = 2
 PIECES = 4
+ROADS = 4
 VMEM_MOST = 60 * 1024 * 1024
 F32, BF16 = jnp.float32, jnp.bfloat16
 
 
 END_UNITS = (
     (0, 1, 2, 3),
-    (4, 5, 17, 18),
-    (21, 8, 6, 16),
-    (20, 24, 12, 10),
-    (25, 28, 14, 19),
-    (26, 29, 30, 31),
-    (22, 27, 13, 15),
-    (23, 9, 11, 7),
+    (18, 4, 7, 16),
+    (9, 17, 19, 5),
+    (13, 15, 20, 23),
+    (28, 29, 25, 12),
+    (30, 31, 24, 27),
+    (26, 14, 11, 22),
+    (8, 21, 10, 6),
 )
 END_MOVES = (
     (
-        (0, 0), (0, 1), (0, 2), (0, 3), (1, 0, 1, 1), (1, 2, 1, 1), (1, 1, 0, 4), (1, 2, 0, 4), (1, 3, 1, 1),
-        (1, 0, 0, 4), (1, 1, 1, 1),
-    ),
-    (
-        (0, 5), (0, 17), (0, 4), (0, 18), (1, 17, 1, 5), (1, 5, 0, 5), (1, 3, 0, 4), (1, 18, 1, 5), (0, 6),
-        (0, 16),
-    ),
-    (
-        (0, 21), (0, 8), (1, 8, 0, 6), (0, 19), (0, 20), (2, 17, 0, 0, 0), (2, 4, 1, 0, 0), (2, 5, 1, 0, 0),
-    ),
-    (
-        (0, 10), (0, 24), (0, 12), (1, 12, 0, 7), (1, 10, 0, 6), (0, 25), (2, 16, 0, 0, 0), (2, 8, 1, 3, 0),
-        (2, 21, 1, 4, 0),
-    ),
-    (
-        (0, 14), (0, 28), (1, 14, 0, 7), (0, 15), (0, 26), (2, 24, 1, 7, 0), (2, 20, 1, 4, 0), (0, 29),
-    ),
-    (
-        (0, 31), (0, 30), (0, 11), (1, 11, 0, 6), (2, 28, 0, 3, 0), (2, 14, 1, 2, 0), (2, 25, 1, 7, 0),
-    ),
-    (
-        (0, 13), (0, 27), (0, 22), (2, 12, 1, 2, 1), (0, 23), (2, 29, 0, 3, 0), (2, 30, 1, 6, 0),
-        (2, 26, 0, 2, 0),
-    ),
-    (
-        (0, 7), (0, 9), (2, 31, 1, 6, 0), (2, 13, 1, 2, 1), (2, 15, 1, 2, 0), (2, 27, 0, 2, 0),
-        (2, 22, 0, 1, 0),
-    ),
-    (
-        (2, 10, 1, 3, 1), (2, 9, 1, 3, 0), (2, 11, 1, 3, 1), (2, 23, 0, 1, 0), (2, 0, 3, 0, 3),
-        (2, 6, 1, 0, 1), (2, 18, 0, 0, 2), (2, 7, 1, 0, 1), (2, 19, 0, 0, 2), (2, 1, 3, 0, 3),
-        (2, 2, 3, 0, 3), (2, 3, 3, 0, 3),
+        (0, 0), (0, 1), (0, 2), (0, 3), (1, 2, 1, 1), (1, 2, 0, 4), (1, 0, 3, 2), (1, 0, 0, 4), (1, 1, 3, 2),
+        (1, 1, 0, 4),
+    ),
+    (
+        (1, 3, 1, 1), (1, 3, 0, 4), (0, 18), (0, 4), (1, 3, 2, 3), (1, 4, 0, 5), (0, 16), (0, 7),
+        (1, 1, 1, 1), (1, 7, 0, 5),
+    ),
+    (
+        (0, 17), (0, 5), (0, 19), (0, 9), (1, 9, 0, 6), (1, 2, 3, 2), (1, 16, 1, 5), (0, 20), (1, 0, 1, 1),
+        (2, 18, 0, 0, 0),
+    ),
+    (
+        (0, 15), (0, 23), (0, 13), (0, 25), (1, 13, 0, 7), (1, 15, 0, 7), (2, 7, 1, 0, 0), (0, 12),
+        (2, 9, 1, 3, 0), (2, 17, 0, 0, 0),
+    ),
+    (
+        (0, 11), (0, 28), (0, 29), (1, 11, 0, 6), (0, 31), (0, 24), (2, 13, 1, 2, 0), (2, 15, 1, 2, 0),
+        (2, 20, 0, 1, 0),
+    ),
+    (
+        (0, 30), (0, 27), (2, 23, 1, 4, 0), (0, 14), (2, 28, 0, 3, 0), (2, 29, 1, 6, 0), (2, 25, 1, 7, 0),
+    ),
+    (
+        (0, 26), (0, 22), (2, 4, 1, 0, 1), (0, 8), (2, 12, 1, 2, 1), (2, 30, 0, 3, 0), (2, 24, 0, 2, 0),
+        (2, 31, 1, 6, 0),
+    ),
+    (
+        (0, 21), (0, 10), (2, 27, 0, 2, 0), (0, 6), (2, 14, 1, 2, 1), (2, 26, 0, 2, 0), (2, 22, 0, 1, 0),
+    ),
+    (
+        (2, 11, 3, 0, 1), (2, 19, 0, 0, 2), (2, 10, 1, 3, 1), (2, 8, 1, 3, 1), (2, 21, 0, 1, 0),
+        (2, 16, 0, 0, 2), (2, 6, 1, 0, 1), (2, 5, 1, 0, 1), (2, 1, 4, 0, 3), (2, 0, 4, 0, 3),
+        (2, 3, 4, 0, 11), (2, 2, 4, 0, 3),
     ),
 )
 INNER_UNITS = (
-    (0, 1, 2, 3),
-    (12, 13, 4, 6),
-    (14, 16, 18, 19),
-    (8, 15, 5, 7),
-    (10, 21, 22, 23),
-    (11, 24, 25, 20),
-    (26, 27, 17, 28),
-    (9, 29, 30, 31),
+    (0, 2, 3, 1),
+    (18, 16, 6, 13),
+    (8, 9, 17, 7),
+    (22, 19, 5, 15),
+    (11, 28, 23, 24),
+    (10, 31, 25, 26),
+    (20, 21, 4, 14),
+    (29, 27, 12, 30),
 )
 INNER_MOVES = (
     (
-        (0, 0), (0, 1), (0, 2), (0, 3), (1, 0, 2, 3), (1, 1, 2, 3), (1, 1, 1, 1), (1, 0, 1, 1), (1, 0, 0, 4),
-        (1, 2, 0, 4), (1, 2, 2, 3), (1, 2, 1, 1), (1, 3, 0, 4), (1, 3, 2, 3),
-    ),
-    (
-        (0, 4), (0, 12), (0, 6), (0, 13), (0, 16), (0, 18), (1, 13, 0, 7), (1, 12, 0, 7), (1, 4, 2, 2),
-        (1, 12, 1, 2), (1, 16, 1, 5), (1, 6, 2, 2), (0, 7), (0, 14), (0, 19), (1, 7, 0, 5), (1, 14, 1, 2),
-    ),
-    (
-        (0, 15), (0, 5), (0, 21), (0, 29), (0, 8), (1, 8, 1, 3), (1, 21, 2, 6), (1, 8, 0, 6), (1, 7, 2, 2),
-        (1, 29, 1, 6), (1, 4, 0, 5),
-    ),
-    (
-        (0, 28), (0, 10), (0, 22), (0, 23), (1, 10, 1, 3), (1, 23, 2, 6), (1, 22, 2, 6), (1, 1, 0, 4),
-    ),
-    (
-        (0, 25), (0, 24), (0, 11), (0, 20), (1, 11, 1, 3), (1, 5, 2, 2), (1, 25, 1, 7), (2, 18, 0, 0, 0),
-    ),
-    (
-        (0, 27), (0, 26), (0, 17), (1, 27, 1, 7), (1, 15, 1, 2), (1, 18, 2, 7), (1, 19, 2, 7),
-    ),
-    (
-        (0, 9), (1, 9, 1, 3), (2, 12, 2, 0, 2), (2, 21, 0, 1, 0),
-    ),
-    (
-        (0, 30), (0, 31), (1, 18, 1, 5), (1, 19, 1, 5), (2, 24, 2, 5, 0), (2, 25, 0, 2, 0), (1, 3, 1, 1),
-        (2, 28, 2, 4, 2), (2, 17, 0, 0, 2),
-    ),
-    (
-        (2, 20, 0, 1, 4), (2, 10, 2, 1, 2), (1, 13, 1, 2), (2, 16, 0, 0, 6), (2, 30, 0, 3, 0),
-        (2, 31, 2, 4, 0), (2, 29, 0, 3, 2), (2, 6, 1, 0, 4), (2, 8, 2, 1, 2), (2, 0, 3, 0, 7),
-        (2, 19, 0, 0, 4), (2, 26, 2, 5, 2), (2, 27, 2, 5, 2), (2, 4, 1, 0, 5), (2, 9, 2, 1, 3),
-        (2, 22, 1, 4, 4), (2, 11, 2, 1, 2), (2, 23, 1, 4, 4), (2, 14, 2, 0, 3), (2, 5, 1, 0, 5),
-        (2, 13, 2, 0, 3), (2, 7, 1, 0, 4), (2, 15, 2, 0, 2), (2, 2, 3, 0, 7), (2, 1, 3, 0, 7),
-        (2, 3, 3, 0, 7),
+        (0, 0), (0, 1), (0, 2), (0, 3), (1, 0, 0, 4), (1, 2, 0, 4), (1, 1, 2, 3), (1, 0, 1, 1), (1, 3, 1, 1),
+        (1, 1, 0, 4), (1, 1, 1, 1),
+    ),
+    (
+        (1, 3, 2, 3), (0, 16), (0, 6), (0, 13), (1, 13, 1, 2), (1, 6, 0, 5), (1, 3, 0, 4), (0, 18), (0, 8),
+        (1, 8, 0, 6), (1, 16, 2, 7),
+    ),
+    (
+        (0, 9), (0, 17), (0, 7), (0, 22), (1, 7, 2, 2), (1, 9, 1, 3), (1, 8, 1, 3), (1, 9, 0, 6),
+        (1, 7, 0, 5), (0, 15), (0, 19), (1, 15, 1, 2), (1, 15, 0, 7),
+    ),
+    (
+        (0, 5), (0, 24), (0, 28), (0, 25), (1, 22, 2, 6), (1, 24, 1, 7), (1, 18, 2, 7), (1, 28, 1, 6),
+        (2, 18, 0, 0, 0), (1, 5, 0, 5), (0, 11), (1, 2, 2, 3), (0, 23), (0, 20),
+    ),
+    (
+        (0, 10), (0, 31), (0, 4), (0, 26), (1, 26, 1, 7), (1, 10, 1, 3), (1, 0, 2, 3), (1, 11, 0, 6),
+    ),
+    (
+        (0, 30), (0, 21), (1, 30, 1, 6), (2, 22, 0, 1, 0), (1, 18, 1, 5), (1, 17, 2, 7), (2, 13, 2, 0, 2),
+        (0, 14),
+    ),
+    (
+        (0, 12), (0, 27), (2, 28, 2, 4, 0), (2, 24, 0, 2, 0), (1, 12, 1, 2), (1, 17, 1, 5),
+    ),
+    (
+        (0, 29), (2, 26, 0, 2, 0), (1, 14, 1, 2), (2, 31, 0, 3, 0), (2, 9, 2, 1, 2), (1, 2, 1, 1),
+        (2, 19, 0, 0, 2),
+    ),
+    (
+        (2, 25, 2, 5, 2), (2, 16, 0, 0, 4), (2, 7, 1, 0, 0), (2, 23, 1, 4, 0), (2, 29, 2, 4, 2),
+        (2, 30, 0, 3, 0), (2, 15, 2, 0, 1), (2, 20, 1, 4, 0), (2, 8, 2, 1, 3), (2, 21, 0, 1, 4),
+        (2, 27, 0, 2, 2), (2, 17, 0, 0, 4), (2, 10, 2, 1, 3), (2, 5, 1, 0, 5), (2, 4, 1, 0, 4),
+        (2, 11, 3, 0, 3), (2, 3, 4, 0, 15), (2, 14, 2, 0, 3), (2, 6, 1, 0, 5), (2, 12, 2, 0, 2),
+        (2, 2, 4, 0, 7), (2, 1, 4, 0, 7), (2, 0, 4, 0, 7),
     ),
 )
 
@@ -176,7 +179,9 @@
         return first + 2 * second
 
     sibling = {"expert": chip * CORES + 1 - core}
-    roads = ({"sub": 1 - sub}, {"expert": place(1) * CORES + core}, {"expert": place(3) * CORES + core})
+    roads = ({"sub": 1 - sub},) + tuple(
+        {"expert": place(step) * CORES + core} for step in (1, 3, 2)
+    )
 
     def send(src, dst, s_sem, r_sem, device):
         return pltpu.make_async_remote_copy(
@@ -237,7 +242,7 @@
 
     def sum_onward(code, road, block):
         spot = block * PIECES + code % PIECES
-        return send(sums_out.at[code], sums_in.at[3 * spot + road], sum_s, sum_r.at[spot, road], roads[road])
+        return send(sums_out.at[code], sums_in.at[ROADS * spot + road], sum_s, sum_r.at[spot, road], roads[road])
 
     def landed(code):
         onward(code, 0, code // PIECES).wait_recv()
@@ -260,13 +265,13 @@
                 part_to_mate(unit).wait_recv()
                 joined.add(unit)
             total = kept[unit, spot] + mate_in[unit, spot].astype(F32)
-            for road in range(len(roads)):
+            for road in range(ROADS):
                 if move[4] >> road & 1:
-                    sum_r_of = send(sums_out.at[code], sums_in.at[3 * code + road], sum_s,
+                    sum_r_of = send(sums_out.at[code], sums_in.at[ROADS * code + road], sum_s,
                                     sum_r.at[code, road], roads[road])
                     sum_r_of.wait_recv()
-                    total = total + sums_in[3 * code + road].astype(F32)
-            if move[2] < len(roads):
+                    total = total + sums_in[ROADS * code + road].astype(F32)
+            if move[2] < ROADS:
                 sums_out[code] = total.astype(BF16)
                 sum_onward(code, *move[2:4]).start()
             else:
@@ -346,7 +351,7 @@
         def _():
             moves = [move for phase in plans[role][1] for move in phase]
             for kind, sem in ((1, far_s), (2, sum_s)):
-                sent = sum(move[0] == kind and move[2] < len(roads) for move in moves)
+                sent = sum(move[0] == kind and move[2] < ROADS for move in moves)
                 whole = sums_in.at[pl.ds(0, sent)]
                 send(whole, whole, sem, sem, roads[0]).wait_send()
 
@@ -379,11 +384,11 @@
             pltpu.VMEM((units, spots, part, width), BF16),
             pltpu.VMEM((units, spots, part, width), BF16),
             pltpu.VMEM((blocks * PIECES, part, width), BF16),
-            pltpu.VMEM((blocks * PIECES * 3, part, width), BF16),
+            pltpu.VMEM((blocks * PIECES * ROADS, part, width), BF16),
             dma((2,)), dma((PIECES,)), dma((2,)),
             dma, dma((lanes * CORES,)), dma, dma,
             dma, dma((blocks * PIECES,)), dma, dma((blocks * PIECES,)),
-            dma, dma((units,)), dma, dma((blocks * PIECES, 3)),
+            dma, dma((units,)), dma, dma((blocks * PIECES, ROADS)),
         ],
         compiler_params=pltpu.CompilerParams(
             collective_id=0, has_side_effects=True, vmem_limit_bytes=VMEM_MOST
@@ -395,7 +400,7 @@
     tokens, width = latent.shape
     experts, subs = lax.axis_size("expert"), lax.axis_size("sub")
     block = tokens * width * 2
-    need = 8 * block * (2 + 2 + 1 + 1 + 1 + 3) + 4 * up_weight.size + 4 * block
+    need = 8 * block * (2 + 2 + 1 + 1 + 1 + ROADS) + 4 * up_weight.size + 4 * block
     fits = subs == 2 and experts == 4 * CORES and need < VMEM_MOST
     plan = grid if fits and tokens % (16 * PIECES) == 0 and tokens % 128 == 0 else routed
     return plan(latent, routes, gates, up_weight, down_weight)

time: 56.1 us -> 54.1 us (0.964)
  Pallas kernels: 54.2 us -> 52.2 us
    pallas_call x1, Pallas kernels: 54.2 us -> 52.2 us  [grid(): pl.pallas_call(grid_kernel, out_shape=jax.ShapeDtypeStruct((tokens, width...]
where the time goes in v2:
time: 54.1 us; the launch traced here: 53.9 us
  Pallas kernels  52.2 us (96%)
  local copies, waits for them, and re-layouts  1.67 us (3%)
    pallas_call x1, Pallas kernels, grid(): pl.pallas_call(grid_kernel, out_shape=jax.ShapeDtypeStruct((tokens, width...  52.2 us
    unnamed x1, local copies, waits for them, and re-layouts  1.67 us

profile of v2, /device:TPU:0, one launch (start us, length us, event | category | flops | bytes accessed | tf_op | source)
XLA Modules:
  0.0 53.9 jit_solution(7681376370458619027)
XLA Ops:
  0.0 52.2 %shard_map.55 = bf16[128,1024]{1,0:T(8,128)(2,1)} custom-call(s32[4,128]{1,0:T(4,128)} %bitcast.6, f32[4,128]{1,0:T(4,128)} %bitcast.7, bf16[128,1024]{1,0:T(8,128)(2,1)} %latent_hbm.1, bf16[1,1344,1024]{2,1,0:T(8,128)(2,1)} %bitcast.4, bf16[1,1344,1024]{2,1,0:T(8,128)(2,1)} %bitcast.5), custom_call_target="tpu_custom_call" | custom-call | tf_op jit(solution)/shard_map/pallas_call | solution.py:370
  52.3 1.7 %copy.7 = bf16[128,1024]{1,0:T(8,128)(2,1)} copy(bf16[128,1024]{1,0:T(8,128)(2,1)} %shard_map.55) | data formatting | bytes 524288
